TPU v7x, 256 devices: a whole 4x4x8 slice. The times are simulated.
256 devices in a mesh: rows: 256 (over y, z, x, core).
Axes of the slice: x: 4, y: 4, z: 8, core: 2. Of those that a mesh axis runs over, the one named last changes fastest.
Arguments:
- features: bfloat16 [1048576, 440], P('rows'), may hold values from -6 to 6
- residual: float32 [1048576], P('rows')
- block_index: int32 [1024], replicated, may hold values from 0 to 1048575, as said below
Outputs:
- updated: float32 [1048576], P('rows')
- coefficient: float32 [1024], replicated
- rms_value: float32 [], replicated
Inputs may be any that keep to these rules, and one draw needn't show every extreme that they name: `block_index`: 1024 distinct frame indices; no device's range of 4096 frames holds more than 8 of them, and some device holds exactly 8.
All inputs are finite; a program needn't handle non-finite values.
Results may differ from a plain program's by a relative error of at most 0.0003.
Values may be sent and summed in bfloat16 or wider, within the bound.
A program may use at most 128 MiB of HBM per device.

v0:
```python
import jax
import jax.numpy as jnp
from jax import lax
from jax.sharding import PartitionSpec as P


def kernel_of(left, right, left_norm, right_norm, scale):
    inner = jnp.dot(left, right.T, preferred_element_type=jnp.float32)
    return jnp.exp(-scale * (left_norm[:, None] + right_norm[None, :] - 2.0 * inner))


def chol_apply(factor, target):
    column = target[:, None]
    forward = lax.linalg.triangular_solve(factor, column, left_side=True, lower=True)
    backward = lax.linalg.triangular_solve(
        factor, forward, left_side=True, lower=True, transpose_a=True
    )
    return backward[:, 0]


def on_device(features, residual, block_index):
    local_rows, width = features.shape
    block_size = block_index.shape[0]
    scale = 2.0 / width
    own_index = lax.axis_index("rows")
    owner = block_index // local_rows
    offset = block_index - owner * local_rows
    mine = owner == own_index
    safe_offset = jnp.where(mine, offset, 0)
    picked = jnp.where(mine[:, None], features[safe_offset].astype(jnp.float32), 0.0)
    picked_res = jnp.where(mine, residual[safe_offset], 0.0)
    summed = lax.psum((picked, picked_res), "rows")
    block_feat = summed[0].astype(jnp.bfloat16)
    block_res = summed[1]
    block_norm = jnp.sum(jnp.square(block_feat.astype(jnp.float32)), axis=1)
    system = kernel_of(block_feat, block_feat, block_norm, block_norm, scale)
    system = system + 0.1 * jnp.eye(block_size, dtype=jnp.float32)
    factor = jnp.linalg.cholesky(system)
    coefficient = chol_apply(factor, block_res)
    block_rows = min(1024, local_rows)
    grouped = features.reshape(local_rows // block_rows, block_rows, width)

    def one_block(rows_in):
        row_norm = jnp.sum(jnp.square(rows_in.astype(jnp.float32)), axis=1)
        panel = kernel_of(rows_in, block_feat, row_norm, block_norm, scale)
        return jnp.dot(panel, coefficient, precision=lax.Precision.HIGHEST)

    change = lax.map(one_block, grouped).reshape(local_rows)
    updated = residual - change
    square_sum = lax.psum(jnp.sum(updated * updated), "rows")
    frame_count = local_rows * lax.axis_size("rows")
    rms_value = jnp.sqrt(square_sum / frame_count + 1e-06)
    return (updated, coefficient, rms_value)


def solution(mesh):
    in_specs = (P("rows", None), P("rows"), P())
    out_specs = (P("rows"), P(), P())
    return jax.shard_map(
        on_device, mesh=mesh, in_specs=in_specs, out_specs=out_specs, check_vma=False
    )
```

profile of v0, /device:TPU:1, one launch (start us, length us, event | category | flops | bytes accessed | tf_op | source)
XLA Modules:
  0.0 620.0 jit_solution(1290120094716985099)
XLA Ops:
  1.3 6.4 %copy.11 = bf16[4096,440]{1,0:T(8,128)(2,1)} copy(bf16[4096,440]{0,1:T(8,128)(2,1)} %param.5) | data formatting | bytes 7208960 | tf_op args[0]
  7.8 6.7 %gather_fusion = bf16[1024,440]{1,0:T(8,128)(2,1)S(1)} fusion(bf16[4096,440]{1,0:T(8,128)(2,1)} %copy.11, s32[1024]{0:T(1024)S(1)} %get-tuple-element.68), kind=kCustom, calls=%fused_computation | custom fusion | bytes 1806336 | tf_op jit(solution)/shard_map/gather | solution.py:30
  14.8 6.2 gather_fusion.1
  20.9 130.4 %all-reduce.3 = (bf16[1024,440]{1,0:T(8,128)(2,1)S(1)}, f32[1024]{0:T(1024)S(1)}) all-reduce(f32[1024,440]{1,0:T(8,128)S(1)} %convert_select_fusion, f32[1024]{0:T(1024)S(1)} %broadcast_select_fusion), channel_id=1, replica_groups=mesh['rows'=256] {'rows'}, use_global_device_ids=true, to_apply=%region_0.1 | all-reduce | flops 451584 | bytes 2711552 | tf_op jit(solution)/shard_map/psum | solution.py:32
  151.7 5.9 multiply_subtract_fusion
  157.6 5.4 copy.14
  163.0 5.4 copy.15
  168.3 6.3 %fusion.20 = f32[1024,1024]{1,0:T(8,128)S(1)} fusion(f32[1024,1024]{1,0:T(8,128)} %copy.15, f32[1024,1024]{1,0:T(8,128)} %copy.14, f32[1024,1024]{0,1:T(8,128)} %get-tuple-element.113), kind=kLoop, calls=%fused_computation.27 | loop fusion | flops 12582912 | bytes 16777216 | tf_op jit(solution)/shard_map/jit(cholesky)/div | solution.py:38
  176.6 11.7 %cholesky.222 = f32[128,128]{1,0:T(8,128)S(1)} custom-call(f32[128,128]{1,0:T(8,128)S(1)} %cholesky.577), custom_call_target="Cholesky" | custom-call | tf_op jit(solution)/shard_map/jit(cholesky)/cholesky | solution.py:38
  188.4 9.8 %custom-call.64 = f32[1,128,128]{1,2,0:T(8,128)S(1)} custom-call(f32[1,128,128]{2,1,0:T(8,128)S(1)} %get-tuple-element.93), custom_call_target="InvertDiagBlocksLowerTriangular" | custom-call | tf_op jit(solution)/shard_map/jit(cholesky)/cholesky | solution.py:38
  198.2 2.5 cholesky.254
  200.7 2.3 constant_dynamic-update-slice_fusion.50
  204.6 11.7 %cholesky.243 = f32[128,128]{1,0:T(8,128)S(1)} custom-call(f32[128,128]{1,0:T(8,128)S(1)} %cholesky.581), custom_call_target="Cholesky" | custom-call | tf_op jit(solution)/shard_map/jit(cholesky)/cholesky | solution.py:38
  218.9 9.9 %custom-call.65 = f32[1,128,128]{1,2,0:T(8,128)S(1)} custom-call(f32[1,128,128]{2,1,0:T(8,128)S(1)} %get-tuple-element.90), custom_call_target="InvertDiagBlocksLowerTriangular" | custom-call | tf_op jit(solution)/shard_map/jit(cholesky)/cholesky | solution.py:38
  232.2 11.7 %cholesky.466 = f32[128,128]{1,0:T(8,128)S(1)} custom-call(f32[128,128]{1,0:T(8,128)S(1)} %cholesky.586), custom_call_target="Cholesky" | custom-call | tf_op jit(solution)/shard_map/jit(cholesky)/cholesky | solution.py:38
  245.9 9.8 %custom-call.66 = f32[1,128,128]{1,2,0:T(8,128)S(1)} custom-call(f32[1,128,128]{2,1,0:T(8,128)S(1)} %get-tuple-element.87), custom_call_target="InvertDiagBlocksLowerTriangular" | custom-call | tf_op jit(solution)/shard_map/jit(cholesky)/cholesky | solution.py:38
  256.8 2.3 convolution_subtract_fusion.2
  259.2 11.9 %cholesky.485 = f32[128,128]{1,0:T(8,128)S(1)} custom-call(f32[128,128]{1,0:T(8,128)S(1)} %cholesky.591), custom_call_target="Cholesky" | custom-call | tf_op jit(solution)/shard_map/jit(cholesky)/cholesky | solution.py:38
  273.0 9.8 %custom-call.67 = f32[1,128,128]{1,2,0:T(8,128)S(1)} custom-call(f32[1,128,128]{2,1,0:T(8,128)S(1)} %get-tuple-element.84), custom_call_target="InvertDiagBlocksLowerTriangular" | custom-call | tf_op jit(solution)/shard_map/jit(cholesky)/cholesky | solution.py:38
  284.0 2.4 convolution_subtract_fusion.3
  286.3 11.7 %cholesky.504 = f32[128,128]{1,0:T(8,128)S(1)} custom-call(f32[128,128]{1,0:T(8,128)S(1)} %cholesky.596), custom_call_target="Cholesky" | custom-call | tf_op jit(solution)/shard_map/jit(cholesky)/cholesky | solution.py:38
  300.0 9.8 %custom-call.68 = f32[1,128,128]{1,2,0:T(8,128)S(1)} custom-call(f32[1,128,128]{2,1,0:T(8,128)S(1)} %get-tuple-element.81), custom_call_target="InvertDiagBlocksLowerTriangular" | custom-call | tf_op jit(solution)/shard_map/jit(cholesky)/cholesky | solution.py:38
  310.8 2.7 convolution_subtract_fusion.4
  313.6 11.7 %cholesky.524 = f32[128,128]{1,0:T(8,128)S(1)} custom-call(f32[128,128]{1,0:T(8,128)S(1)} %cholesky.601), custom_call_target="Cholesky" | custom-call | tf_op jit(solution)/shard_map/jit(cholesky)/cholesky | solution.py:38
  327.2 9.8 %custom-call.69 = f32[1,128,128]{1,2,0:T(8,128)S(1)} custom-call(f32[1,128,128]{2,1,0:T(8,128)S(1)} %get-tuple-element.78), custom_call_target="InvertDiagBlocksLowerTriangular" | custom-call | tf_op jit(solution)/shard_map/jit(cholesky)/cholesky | solution.py:38
  340.0 11.7 %cholesky.544 = f32[128,128]{1,0:T(8,128)S(1)} custom-call(f32[128,128]{1,0:T(8,128)S(1)} %cholesky.606), custom_call_target="Cholesky" | custom-call | tf_op jit(solution)/shard_map/jit(cholesky)/cholesky | solution.py:38
  353.7 9.9 %custom-call.70 = f32[1,128,128]{1,2,0:T(8,128)S(1)} custom-call(f32[1,128,128]{2,1,0:T(8,128)S(1)} %get-tuple-element.75), custom_call_target="InvertDiagBlocksLowerTriangular" | custom-call | tf_op jit(solution)/shard_map/jit(cholesky)/cholesky | solution.py:38
  366.3 11.7 %cholesky.562 = f32[128,128]{1,0:T(8,128)S(1)} custom-call(f32[128,128]{1,0:T(8,128)S(1)} %convolution_subtract_fusion.6), custom_call_target="Cholesky" | custom-call | tf_op jit(solution)/shard_map/jit(cholesky)/cholesky | solution.py:38
  379.9 4.8 select_select_fusion
  384.8 23.2 %while.12 = (s32[]{:T(128)}, f32[1024,1024]{1,0:T(8,128)}, s32[8,2]{0,1:T(2,128)S(1)}, f32[8,128,128]{2,1,0:T(8,128)S(1)}, s32[]{:T(128)}) while((s32[]{:T(128)}, f32[1024,1024]{1,0:T(8,128)}, s32[8,2]{0,1:T(2,128)S(1)}, f32[8,128,128]{2,1,0:T(8,128)S(1)}, s32[]{:T(128)}) %tuple.77), condition=%wide.while_cond, body=%wide.while_body.sunk | while | flops 2 | bytes 131181 | solution.py:15
  385.4 2.3 bitcast_dynamic-update-slice_fusion.2
  388.3 2.3 bitcast_dynamic-update-slice_fusion.2
  391.2 2.3 bitcast_dynamic-update-slice_fusion.2
  394.1 2.3 bitcast_dynamic-update-slice_fusion.2
  397.0 2.3 bitcast_dynamic-update-slice_fusion.2
  399.9 2.3 bitcast_dynamic-update-slice_fusion.2
  402.8 2.3 bitcast_dynamic-update-slice_fusion.2
  408.0 78.8 %custom-call.71 = f32[8,128,128]{1,2,0:T(8,128)S(1)} custom-call(f32[8,128,128]{2,1,0:T(8,128)S(1)} %get-tuple-element.43), custom_call_target="InvertDiagBlocksLowerTriangular" | custom-call | tf_op jit(solution)/shard_map/triangular_solve | solution.py:15
  507.8 34.5 %while.11 = (s32[]{:T(128)}, f32[4,1024]{1,0:T(4,128)S(1)}, bf16[4,1024,440]{2,1,0:T(8,128)(2,1)}, f32[1024]{0:T(1024)S(1)}, bf16[1024,440]{1,0:T(8,128)(2,1)S(1)}, /*index=5*/f32[1024]{0:T(1024)S(1)}, s32[]{:T(128)}, s32[]{:T(128)}) while((s32[]{:T(128)}, f32[4,1024]{1,0:T(4,128)S(1)}, bf16[4,1024,440]{2,1,0:T(8,128)(2,1)}, ...), condition=%wide.region_21.22_spmd, body=%wide.region_19.21_spmd.sunk | while | flops 940874752 | bytes 11268701 | solution.py:48
  507.8 2.5 fusion.181
  511.8 4.5 fusion.182
  516.4 2.5 fusion.181
  520.5 4.5 fusion.182
  525.0 2.5 fusion.181
  529.1 4.5 fusion.182
  533.7 2.5 fusion.181
  537.7 4.5 fusion.182
  543.5 74.4 %psum.23 = f32[]{:T(128)} all-reduce(f32[]{:T(128)} %get-tuple-element.66), channel_id=1, replica_groups=mesh['rows'=256] {'rows'}, use_global_device_ids=true, to_apply=%region_23.24 | all-reduce | flops 1 | bytes 8 | tf_op jit(solution)/shard_map/psum | solution.py:50
  (124 shorter events, 61.5 us)
Async XLA Ops:
  7.8 7.0 %copy-start = (f32[4096]{0:T(1024)S(1)}, f32[4096]{0:T(1024)}, u32[]{:S(2)}) copy-start(f32[4096]{0:T(1024)} %param.6) | copy-start | bytes 49156
  174.6 2.0 copy-start.1
  542.3 76.3 %copy-start.2 = (f32[1024]{0:T(1024)}, f32[1024]{0:T(1024)S(1)}, u32[]{:S(2)}) copy-start(f32[1024]{0:T(1024)S(1)} %get-tuple-element.238) | copy-start | bytes 12292
where the time goes:
time: 627 us; the launch traced here: 620 us
  other arithmetic  270 us (43%)
  blocking collectives  205 us (33%)
  matrix products  78.1 us (12%)
  local copies, waits for them, and re-layouts  58.2 us (9%)
  between operations  8.28 us (1%)
    another operation x30, other arithmetic, on_device(): factor = jnp.linalg.cholesky(system)  172 us
    psum x1, blocking collectives, on_device(): summed = lax.psum((picked, picked_res), 'rows')  130 us
    another operation x3, other arithmetic, chol_apply(): lax.linalg.triangular_solve(factor, forward, left_side=True, lower=True,...  83.6 us
    psum x1, blocking collectives, on_device(): square_sum = lax.psum(jnp.sum(updated * updated), 'rows')  74.4 us
    another operation x14, matrix products, on_device(): factor = jnp.linalg.cholesky(system)  23.5 us
    another operation x24, local copies, waits for them, and re-layouts  23 us
    dot_general x4, matrix products, one_block(): return jnp.dot(panel, coefficient, precision=lax.Precision.HIGHEST)  18 us
    dot_general x5, matrix products, kernel_of(): inner = jnp.dot(left, right.T, preferred_element_type=jnp.float32)  16 us

commit v1 on v0

v1 whole, which is shorter than its diff:
```python
import functools

import jax
import jax.numpy as jnp
from jax import lax
from jax.experimental import pallas as pl
from jax.experimental.pallas import tpu as pltpu
from jax.sharding import PartitionSpec as P

F32 = jnp.float32
BF16 = jnp.bfloat16
LANES = 128
MOST = 8
WIDE = 512
LOG2E = 1.4426950408889634


def pieces(value):
    high = value.astype(BF16).astype(F32)
    rest = value - high
    mid = rest.astype(BF16).astype(F32)
    low = (rest - mid).astype(BF16).astype(F32)
    return high, mid, low


def lane_of(shape):
    return lax.broadcasted_iota(jnp.int32, shape, 1)


def eye_mask():
    return lax.broadcasted_iota(jnp.int32, (LANES, LANES), 0) == lane_of((LANES, LANES))


def to_column(row, eye):
    return jnp.sum(jnp.where(eye, row, 0.0), axis=1, keepdims=True)


def to_row(column, eye):
    return jnp.sum(jnp.where(eye, column, 0.0), axis=0, keepdims=True)


def total(value):
    return jnp.sum(jnp.sum(value, axis=1, keepdims=True), axis=0, keepdims=True)


def solve_kernel(local_rows, width, scale, shift, idx_ref, g_ref, b_ref, coef_ref, place, system):
    size = b_ref.shape[0]
    groups = size // LANES
    slots = g_ref.shape[0]
    base = WIDE - LANES
    col = width - base
    eye = eye_mask()
    owner = (idx_ref[...] // local_rows).astype(F32)
    lower = lane_of((LANES, LANES)) < lax.broadcasted_iota(jnp.int32, (LANES, LANES), 0)
    for t in range(groups):
        mine = to_column(owner[t : t + 1, :], eye)
        count = jnp.where((mine == owner[t : t + 1, :]) & lower, 1.0, 0.0)
        for u in range(t):
            count = count + jnp.where(mine == owner[u : u + 1, :], 1.0, 0.0)
        slot = mine * MOST + jnp.sum(count, axis=1, keepdims=True)
        slot = slot.astype(jnp.int32)
        place[t * LANES : (t + 1) * LANES, :] = jnp.where(
            lane_of((LANES, slots)) == slot, 1.0, 0.0
        ).astype(BF16)
    block = jnp.dot(place[...], g_ref[...], preferred_element_type=F32)
    tail = block[:, base:]
    lane = lane_of(tail.shape)
    target_cols = jnp.sum(
        jnp.where((lane >= col + 6) & (lane < col + 9), tail, 0.0), axis=1, keepdims=True
    )
    tail = jnp.where(lane < col + 6, tail, 0.0)
    moved = pltpu.roll(tail, 3, 1)
    swap = jnp.where(lane < col, tail, jnp.where(lane < col + 3, 1.0, jnp.where(lane < col + 6, moved, 0.0)))
    b_ref[:, :base] = block[:, :base].astype(BF16)
    b_ref[:, base:] = tail.astype(BF16)
    place[:, :base] = block[:, :base].astype(BF16)
    place[:, base:WIDE] = swap.astype(BF16)
    inner = lax.dot_general(
        b_ref[...], place[:, :WIDE], (((1,), (1,)), ((), ())), preferred_element_type=F32
    )
    system[...] = jnp.exp2(inner * (2.0 * scale * LOG2E))
    for t in range(groups):
        here = slice(t * LANES, (t + 1) * LANES)
        system[here, here] = system[here, here] + jnp.where(eye, shift, 0.0)

    target = jnp.concatenate(
        [to_row(target_cols[t * LANES : (t + 1) * LANES], eye) for t in range(groups)], axis=0
    )
    top = jnp.max(jnp.max(jnp.abs(target), axis=1, keepdims=True), axis=0, keepdims=True)
    top = jnp.where(top > 0.0, top, 1.0)
    target = target / top

    def apply(p):
        rows = []
        for t in range(groups):
            acc = system[t * LANES : (t + 1) * LANES, :LANES] * p[:1, :]
            for u in range(1, groups):
                acc = acc + system[t * LANES : (t + 1) * LANES, u * LANES : (u + 1) * LANES] * p[u : u + 1, :]
            rows.append(to_row(jnp.sum(acc, axis=1, keepdims=True), eye))
        return jnp.concatenate(rows, axis=0)

    first = total(target * target)
    bound = first * 1e-12

    def going(carry):
        step, _, _, _, norm = carry
        return (step < 4 * size) & (jnp.sum(norm - bound) > 0.0)

    def advance(carry):
        step, x, r, p, norm = carry
        q = apply(p)
        alpha = norm / total(p * q)
        x = x + alpha * p
        r = r - alpha * q
        fresh = total(r * r)
        p = r + (fresh / norm) * p
        return step + 1, x, r, p, fresh

    out = lax.while_loop(
        going, advance, (jnp.int32(0), jnp.zeros_like(target), target, target, first)
    )
    coef_ref[...] = out[1] * top


def widen(rows):
    width = rows.shape[1]
    base = WIDE - LANES
    col = width - base
    value = rows.astype(F32)
    square = value * value
    parts = square[:, :LANES]
    for t in range(1, base // LANES):
        parts = parts + square[:, t * LANES : (t + 1) * LANES]
    tail = jnp.concatenate(
        [value[:, base:], jnp.zeros((rows.shape[0], LANES - col), F32)], axis=1
    )
    parts = parts + tail * tail
    half = -0.5 * jnp.sum(parts, axis=1, keepdims=True)
    high, mid, low = pieces(half)
    lane = lane_of(tail.shape)
    extra = jnp.where(
        lane < col + 3,
        1.0,
        jnp.where(lane == col + 3, high, jnp.where(lane == col + 4, mid, jnp.where(lane == col + 5, low, 0.0))),
    )
    return jnp.where(lane < col, tail, extra).astype(BF16)


def panel_kernel(tile, scale, coef_ref, b_ref, x_ref, res_ref, out_ref, sum_ref, wide, columns):
    rows, width = x_ref.shape
    size = b_ref.shape[0]
    base = WIDE - LANES
    eye = eye_mask()
    for t in range(size // LANES):
        columns[t * LANES : (t + 1) * LANES, :] = jnp.broadcast_to(
            to_column(coef_ref[t : t + 1, :], eye), (LANES, LANES)
        )

    def step(i, _):
        here = pl.ds(pl.multiple_of(i * tile, tile), tile)
        wide[:, :base] = x_ref[here, :base]
        wide[:, base:] = widen(x_ref[here, :])
        inner = lax.dot_general(
            b_ref[...], wide[...], (((1,), (1,)), ((), ())), preferred_element_type=F32
        )
        value = jnp.exp2(inner * (2.0 * scale * LOG2E))
        for k in range(tile // LANES):
            change = jnp.sum(value[:, k * LANES : (k + 1) * LANES] * columns[...], axis=0, keepdims=True)
            at = pl.ds(i * (tile // LANES) + k, 1)
            out_ref[at, :] = res_ref[at, :] - change
        return 0

    lax.fori_loop(0, rows // tile, step, 0)
    updated = out_ref[...]
    square = updated * updated
    parts = square[:8, :]
    for t in range(1, square.shape[0] // 8):
        parts = parts + square[t * 8 : (t + 1) * 8, :]
    sum_ref[...] = jnp.broadcast_to(total(parts), sum_ref.shape)


VM = pl.BlockSpec(memory_space=pltpu.VMEM)


def solve(idx, gathered, local_rows, width, scale):
    size = idx.shape[0]
    return pl.pallas_call(
        functools.partial(solve_kernel, local_rows, width, scale, 0.1),
        out_shape=(
            jax.ShapeDtypeStruct((size, WIDE), BF16),
            jax.ShapeDtypeStruct((size // LANES, LANES), F32),
        ),
        in_specs=[VM, VM],
        out_specs=(VM, VM),
        scratch_shapes=[
            pltpu.VMEM((size, gathered.shape[0]), BF16),
            pltpu.VMEM((size, size), F32),
        ],
        compiler_params=pltpu.CompilerParams(vmem_limit_bytes=40 << 20),
        name="solve",
    )(idx.reshape(size // LANES, LANES), gathered)


def panel(coef, block, features, residual, scale):
    rows, width = features.shape
    size = block.shape[0]
    tile = 256
    return pl.pallas_call(
        functools.partial(panel_kernel, tile, scale),
        out_shape=(
            jax.ShapeDtypeStruct((rows // LANES, LANES), F32),
            jax.ShapeDtypeStruct((8, LANES), F32),
        ),
        in_specs=[VM, VM, VM, VM],
        out_specs=(VM, VM),
        scratch_shapes=[
            pltpu.VMEM((tile, WIDE), BF16),
            pltpu.VMEM((size, LANES), F32),
        ],
        compiler_params=pltpu.CompilerParams(vmem_limit_bytes=40 << 20),
        name="panel",
    )(coef, block, features, residual.reshape(rows // LANES, LANES))


def rounded(value):
    return lax.reduce_precision(value, 8, 7)


def slots_of(features, residual, block_index):
    local_rows, width = features.shape
    own = lax.axis_index("rows")
    mine = block_index // local_rows == own
    rank = jnp.cumsum(mine.astype(jnp.int32)) - 1
    hit = mine[None, :] & (rank[None, :] == jnp.arange(MOST)[:, None])
    offset = jnp.sum(jnp.where(hit, (block_index - own * local_rows)[None, :], 0), axis=1)
    found = jnp.any(hit, axis=1)[:, None]
    rows = jnp.where(found, features[offset].astype(F32), 0.0)
    res = jnp.where(found, residual[offset][:, None], 0.0)
    half = -0.5 * jnp.sum(rows * rows, axis=1, keepdims=True)

    def split(value):
        high = rounded(value)
        mid = rounded(value - high)
        return [high, mid, rounded(value - high - mid)]

    ones = jnp.where(found, jnp.ones((MOST, 3), F32), 0.0)
    return jnp.concatenate(
        [rows] + split(half) + [ones] + split(res) + [jnp.zeros((MOST, WIDE - width - 9), F32)], axis=1
    ).astype(BF16)


def on_device(features, residual, block_index):
    local_rows, width = features.shape
    scale = 2.0 / width
    mine = slots_of(features, residual, block_index)
    gathered = lax.all_gather(mine, "rows", axis=0, tiled=True)
    block, coef = solve(block_index, gathered, local_rows, width, scale)
    updated, square = panel(coef, block, features, residual, scale)
    square_sum = lax.psum(square[0, 0], "rows")
    frame_count = local_rows * lax.axis_size("rows")
    rms_value = jnp.sqrt(square_sum / frame_count + 1e-06)
    return (updated.reshape(local_rows), coef.reshape(-1), rms_value)


def solution(mesh):
    in_specs = (P("rows", None), P("rows"), P())
    out_specs = (P("rows"), P(), P())
    return jax.shard_map(
        on_device, mesh=mesh, in_specs=in_specs, out_specs=out_specs, check_vma=False
    )
```

time: 627 us -> 252 us (0.40); the launches traced: 620 us -> 252 us
  other arithmetic: 270 us -> 2.25 us
  blocking collectives: 205 us -> 76.9 us
  waiting for transfers between devices: 0 us -> 108 us
  matrix products: 78.1 us -> 0 us
  local copies, waits for them, and re-layouts: 58.2 us -> 17.2 us
  Pallas kernels: 0 us -> 30.8 us
  between operations: 8.28 us -> 15.9 us
    another operation x33 -> x4, other arithmetic: 256 us -> 1.02 us  [the longest x30 172 us: on_device(): factor = jnp.linalg.cholesky(system)]
    psum x2 -> x1, blocking collectives: 205 us -> 76.9 us  [on_device(): square_sum = lax.psum(square[0, 0], 'rows')]
    all_gather x0 -> x1, waiting for transfers between devices: none -> 108 us  [on_device(): gathered = lax.all_gather(mine, 'rows', axis=0, tiled=True)]
    another operation x44 -> x0, matrix products: 44.1 us -> none  [the longest x14 23.5 us: on_device(): factor = jnp.linalg.cholesky(system)]
    dot_general x9 -> x0, matrix products: 34 us -> none  [the longest x4 18 us: one_block(): return jnp.dot(panel, coefficient, precision=lax.Precision.HIGHEST)]
    pallas_call x0 -> x2, Pallas kernels: none -> 30.8 us  [the longest x1 20.5 us: solve(): pl.pallas_call(functools.partial(solve_kernel, local_rows, width, scale,...]
    another operation x37 -> x1, local copies, waits for them, and re-layouts: 25.6 us -> 0.12 us
    gather x2, local copies, waits for them, and re-layouts: 12.9 us -> 4.66 us  [the longest x1 3.3 us: slots_of(): rows = jnp.where(found, features[offset].astype(F32), 0.0)]
  transfers between devices with their start and end apart: 0 -> 1, of which waited for: 0 -> 1; matrix products, arithmetic and copies ran while one was open for 0% -> 0% of each run, Pallas kernels for 0% -> 0%
where the time goes in v1:
time: 252 us
  waiting for transfers between devices  108 us (43%)
  blocking collectives  76.9 us (31%)
  Pallas kernels  30.8 us (12%)
  local copies, waits for them, and re-layouts  17.2 us (7%)
  between operations  15.9 us (6%)
    all_gather x1, waiting for transfers between devices, on_device(): gathered = lax.all_gather(mine, 'rows', axis=0, tiled=True)  108 us
    psum x1, blocking collectives, on_device(): square_sum = lax.psum(square[0, 0], 'rows')  76.9 us
    pallas_call x1, Pallas kernels, solve(): pl.pallas_call(functools.partial(solve_kernel, local_rows, width, scale,...  20.5 us
    unnamed x11, local copies, waits for them, and re-layouts  10.9 us
    pallas_call x1, Pallas kernels, panel(): pl.pallas_call(functools.partial(panel_kernel, tile, scale), out_shape=(j...  10.3 us
  transfers between devices with their start and end apart: 1, of which 1 were waited for; matrix products, arithmetic and copies ran while one was open for 0% of the time, Pallas kernels for 0%

profile of v1, /device:TPU:1, one launch (start us, length us, event | category | flops | bytes accessed | tf_op | source)
XLA Modules:
  0.0 251.5 jit_solution(4749020356276662344)
XLA Ops:
  7.2 0.0 all-gather.2.cloned.1.call-start
  7.2 0.7 convert_bitcast_fusion
  7.9 0.7 broadcast_subtract_fusion
  8.6 0.3 reduce-window.9
  8.9 0.1 slice.10
  9.0 0.1 slice_reduce_fusion
  9.1 0.1 add_bitcast_fusion
  9.2 0.1 fusion.1
  9.3 0.1 select_reduce_fusion
  9.5 0.0 copy-start.3
  9.5 1.4 gather_fusion.1
  10.8 0.1 copy.21
  10.9 0.0 copy-start
  10.9 6.4 %copy.18.x_ref = bf16[4096,440]{1,0:T(8,128)(2,1)} copy(bf16[4096,440]{0,1:T(8,128)(2,1)} %param.3) | data formatting | bytes 7208960 | tf_op args[0]
  17.3 3.3 %gather_fusion = bf16[8,440]{1,0:T(8,128)(2,1)S(1)} fusion(bf16[4096,440]{1,0:T(8,128)(2,1)} %copy.18.x_ref, s32[1024]{0:T(1024)S(1)} %pad_clamp_fusion), kind=kCustom, calls=%fused_computation | custom fusion | bytes 14112 | tf_op jit(solution)/shard_map/gather | solution.py:237
  20.6 0.2 multiply_reduce_fusion
  20.8 0.1 copy.19
  20.9 0.1 broadcast_in_dim.55
  21.0 0.7 concatenate.4
  21.7 0.0 all-gather.2.cloned.1.call-update
  21.7 108.5 %all-gather.2.cloned.1.call-done.g_ref = bf16[2048,512]{1,0:T(8,128)(2,1)} async-done(((bf16[8,512]{1,0:T(8,128)(2,1)}), bf16[2048,512]{1,0:T(8,128)(2,1)}) %all-gather.2.cloned.1.call-update) | async-done | bytes 2097168 | tf_op jit(solution)/shard_map/all_gather | solution.py:256
  130.2 0.0 copy-done.3
  130.2 0.0 copy-start.2
  130.2 1.6 copy-done.2
  131.8 20.5 %solve.1 = (bf16[1024,512]{1,0:T(8,128)(2,1)S(1)}, f32[8,128]{1,0:T(8,128)}) custom-call(s32[8,128]{1,0:T(8,128)S(1)} %bitcast.18, bf16[2048,512]{1,0:T(8,128)(2,1)S(1)} %copy-done.2), custom_call_target="tpu_custom_call" | custom-call | tf_op jit(solution)/shard_map/solve/pallas_call | solution.py:187
  152.3 0.0 copy-done
  152.3 0.0 copy-start.1
  152.3 2.2 copy-done.1
  154.5 0.0 copy-start.4
  154.5 0.7 copy-done.4
  155.2 10.3 %panel.1 = (f32[32,128]{1,0:T(8,128)}, f32[8,128]{1,0:T(8,128)S(1)}) custom-call(f32[8,128]{1,0:T(8,128)S(1)} %copy-done.4, bf16[1024,512]{1,0:T(8,128)(2,1)S(1)} %get-tuple-element.8.b_ref, bf16[4096,440]{1,0:T(8,128)(2,1)S(1)} %copy-done.1, f32[32,128]{1,0:T(8,128)S(1)} %bitcast.17), custom_call_target="tpu_custom_call" | custom-call | tf_op jit(solution)/shard_map/panel/pallas_call | solution.py:208
  165.5 0.5 slice.12
  166.0 76.9 %psum.7 = f32[]{:T(128)} all-reduce(f32[]{:T(128)} %bitcast.10), channel_id=1, replica_groups=mesh['rows'=256] {'rows'}, use_global_device_ids=true, to_apply=%region_5.6 | all-reduce | flops 1 | bytes 8 | tf_op jit(solution)/shard_map/psum | solution.py:259
  (7 shorter events, 0.1 us)
Async XLA Ops:
  7.2 123.0 %all-gather.2.cloned.1.call-start = ((), (), s32[]{:S(2)}) async-start(), calls=%async_computation | async-start | bytes 2105344 | tf_op jit(solution)/shard_map/all_gather | solution.py:256
  9.5 120.7 %copy-start.3 = (s32[1024]{0:T(1024)S(1)}, s32[1024]{0:T(1024)}, u32[]{:S(2)}) copy-start(s32[1024]{0:T(1024)} %param.5) | copy-start | bytes 12292
  10.9 141.4 %copy-start = (f32[4096]{0:T(1024)S(1)}, f32[4096]{0:T(1024)}, u32[]{:S(2)}) copy-start(f32[4096]{0:T(1024)} %param.4) | copy-start | bytes 49156
  130.2 1.6 copy-start.2
  152.3 2.2 copy-start.1
  154.5 0.7 copy-start.4
Sparse Core Ops, SparseCore 0:
  21.8 108.2 all-gather.1

commit v2 on v1

v2 whole, which is shorter than its diff:
```python
import functools

import jax
import jax.numpy as jnp
from jax import lax
from jax.experimental import pallas as pl
from jax.experimental.pallas import tpu as pltpu
from jax.sharding import PartitionSpec as P

F32 = jnp.float32
BF16 = jnp.bfloat16
LANES = 128
MOST = 8
WIDE = 512
LOG2E = 1.4426950408889634
GRID = (4, 8, 4)
DEEP = 448
MESH = pl.DeviceIdType.MESH


def pieces(value):
    high = value.astype(BF16).astype(F32)
    rest = value - high
    mid = rest.astype(BF16).astype(F32)
    low = (rest - mid).astype(BF16).astype(F32)
    return high, mid, low


def lane_of(shape):
    return lax.broadcasted_iota(jnp.int32, shape, 1)


def eye_mask():
    return lax.broadcasted_iota(jnp.int32, (LANES, LANES), 0) == lane_of((LANES, LANES))


def to_column(row, eye):
    return jnp.sum(jnp.where(eye, row, 0.0), axis=1, keepdims=True)


def to_row(column, eye):
    return jnp.sum(jnp.where(eye, column, 0.0), axis=0, keepdims=True)


def total(value):
    return jnp.sum(jnp.sum(value, axis=1, keepdims=True), axis=0, keepdims=True)


def position():
    me = lax.axis_index("rows")
    core = lax.rem(me, 2)
    x = lax.rem(me // 2, GRID[2])
    z = lax.rem(me // (2 * GRID[2]), GRID[1])
    y = me // (2 * GRID[2] * GRID[1])
    return me, y, z, x, core


def device(y, z, x, core):
    return ((y * GRID[1] + z) * GRID[2] + x) * 2 + core


def signal(barrier, target):
    pl.semaphore_signal(barrier, inc=1, device_id=(target,), device_id_type=MESH)


def send_to(src, dst, send_sem, recv_sem, target):
    return pltpu.make_async_remote_copy(
        src_ref=src, dst_ref=dst, send_sem=send_sem, recv_sem=recv_sem,
        device_id=(target,), device_id_type=MESH,
    )


def own_offsets(idx, me, local_rows):
    size = idx.shape[0] * LANES
    mine = jnp.where(idx // local_rows == me, 1.0, 0.0)
    sub = lax.broadcasted_iota(jnp.int32, (LANES, LANES), 0)
    before = jnp.where(sub < lane_of((LANES, LANES)), 1.0, 0.0)
    rank = jnp.dot(mine, before, preferred_element_type=F32)
    count = jnp.sum(mine, axis=1, keepdims=True)
    row = lax.broadcasted_iota(jnp.int32, idx.shape, 0)
    for t in range(idx.shape[0] - 1):
        rank = rank + jnp.where(row > t, count[t : t + 1, :], 0.0)
    offset = (idx - me * local_rows + 1).astype(F32)
    return [
        total(jnp.where((mine > 0.0) & (rank == s), offset, 0.0)) - 1.0 for s in range(MOST)
    ]


def stacked(values):
    sub = lax.broadcasted_iota(jnp.int32, (MOST, 1), 0)
    out = jnp.broadcast_to(values[0], (MOST, 1))
    for s in range(1, MOST):
        out = jnp.where(sub == s, values[s], out)
    return out


def gather_kernel(
    local_rows, idx_ref, x_hbm, res_ref, xa_ref, block_ref,
    xs, place, pair, own, other, load_sem, pair_sem, far_send, far_recv, two_send, two_recv,
    three_send, three_recv, relay_send, relay_recv, swap_send, swap_recv,
):
    width = xs.shape[0]
    size = block_ref.shape[0]
    base = WIDE - LANES
    half = WIDE // 2
    chunks = load_sem.shape[0]
    step = local_rows // chunks
    me, y, z, x, core = position()
    two = core * y + (1 - core) * x
    three = core * x + (1 - core) * y
    ring = GRID[0]
    deep = GRID[1]
    partner = device(y, z, x, 1 - core)

    def on_z(v):
        return device(y, v, x, core)

    def on_two(v):
        return device(core * v + (1 - core) * y, z, core * x + (1 - core) * v, core)

    def on_three(v):
        return device(core * y + (1 - core) * v, z, core * v + (1 - core) * x, core)

    def turn(v, by, n):
        return lax.rem(v + by + n, n)

    plus, minus = on_three(turn(three, 1, ring)), on_three(turn(three, -1, ring))

    barrier = pltpu.get_barrier_semaphore()
    signal(barrier, partner)
    for d in range(1, deep):
        signal(barrier, on_z(turn(z, d, deep)))
    for d in range(1, ring):
        signal(barrier, on_two(turn(two, d, ring)))
    signal(barrier, plus)
    signal(barrier, minus)

    loads = []
    for c in range(chunks):
        here = slice(c * step, (c + 1) * step)
        loads.append(pltpu.make_async_copy(x_hbm.at[:, here], xs.at[:, here], load_sem.at[c]))
        loads[-1].start()

    idx = idx_ref[...]
    offsets = own_offsets(idx, me, local_rows)
    column = stacked(offsets)
    frame = (
        lax.broadcasted_iota(jnp.int32, res_ref.shape, 0) * LANES + lane_of(res_ref.shape)
    ).astype(F32)
    target = stacked([total(jnp.where(frame == v, res_ref[...], 0.0)) for v in offsets])
    rows = None
    for c in range(chunks):
        loads[c].wait()
        hot = jnp.where(
            lane_of((MOST, step)).astype(F32) + float(c * step) == column, 1.0, 0.0
        ).astype(BF16)
        part = lax.dot_general(
            hot, xs[:, c * step : (c + 1) * step], (((1,), (1,)), ((), ())),
            preferred_element_type=F32,
        )
        rows = part if rows is None else rows + part
    col = width - base
    tail = jnp.concatenate([rows[:, base:], jnp.zeros((MOST, LANES - col), F32)], axis=1)
    square = tail * tail
    for t in range(base // LANES):
        square = square + rows[:, t * LANES : (t + 1) * LANES] * rows[:, t * LANES : (t + 1) * LANES]
    norm = pieces(-0.5 * jnp.sum(square, axis=1, keepdims=True))
    wanted = pieces(target)
    lane = lane_of(tail.shape)
    for k in range(3):
        tail = jnp.where(lane == col + k, norm[k], tail)
        tail = jnp.where(lane == col + 3 + k, 1.0, tail)
        tail = jnp.where(lane == col + 6 + k, wanted[k], tail)
    pair[core, :, :base] = rows[:, :base]
    pair[core, :, base:] = tail

    pl.semaphore_wait(barrier, 1 + (deep - 1) + (ring - 1) + 2)

    first = send_to(pair.at[core], pair.at[core], pair_sem.at[0], pair_sem.at[1], partner)
    first.start()
    first.wait()
    mine = pl.ds(pl.multiple_of(core * half, half), half)
    both = jnp.concatenate([pair[0, :, mine], pair[1, :, mine]], axis=0)
    own[three, two, z] = both.astype(BF16)

    waits = []
    far = []
    for d in range(1, deep):
        there = own.at[three, two, z]
        far.append(send_to(there, there, far_send.at[d - 1], far_recv.at[d - 1], on_z(turn(z, d, deep))))
        far[-1].start()
    waits += far

    eye = eye_mask()
    owner = idx // local_rows
    row_owner = owner.astype(F32)
    home = lax.rem(owner, 2) * MOST + lax.rem(owner // (2 * GRID[2]), deep) * (2 * MOST)
    on_x = lax.rem(owner // 2, GRID[2])
    on_y = owner // (2 * GRID[2] * deep)
    spans = (2 * MOST * deep * ring, 2 * MOST * deep)
    slot_own = (home + (core * on_x + (1 - core) * on_y) * spans[0] + (core * on_y + (1 - core) * on_x) * spans[1]).astype(F32)
    slot_other = (home + (core * on_y + (1 - core) * on_x) * spans[0] + (core * on_x + (1 - core) * on_y) * spans[1]).astype(F32)
    lower = lane_of((LANES, LANES)) < lax.broadcasted_iota(jnp.int32, (LANES, LANES), 0)
    slots = place.shape[2]
    for t in range(size // LANES):
        here = slice(t * LANES, (t + 1) * LANES)
        holder = to_column(row_owner[t : t + 1, :], eye)
        count = jnp.where((holder == row_owner[t : t + 1, :]) & lower, 1.0, 0.0)
        for u in range(t):
            count = count + jnp.where(holder == row_owner[u : u + 1, :], 1.0, 0.0)
        rank = jnp.sum(count, axis=1, keepdims=True)
        for k, slot in enumerate((slot_own, slot_other)):
            at = (to_column(slot[t : t + 1, :], eye) + rank).astype(jnp.int32)
            place[k, here, :] = jnp.where(lane_of((LANES, slots)) == at, 1.0, 0.0).astype(BF16)

    def widen(c):
        here = slice(c * step, (c + 1) * step)
        value = xs[:, here].astype(F32)
        square = value * value
        parts = square[:8, :]
        for t in range(1, width // 8):
            parts = parts + square[t * 8 : (t + 1) * 8, :]
        norm = pieces(-0.5 * jnp.sum(parts, axis=0, keepdims=True))
        sub = lax.broadcasted_iota(jnp.int32, (8, step), 0)
        extra = jnp.where(sub < 3, 1.0, 0.0)
        for k in range(3):
            extra = jnp.where(sub == 3 + k, norm[k], extra)
        xa_ref[: width - 8, here] = xs[: width - 8, here]
        xa_ref[width - 8 :, here] = jnp.concatenate([value[width - 8 :, :], extra], axis=0).astype(BF16)

    other_cols = pl.ds(pl.multiple_of((1 - core) * half, half), half)

    def add_block(which, index, start):
        buf, cols = (own, mine) if which == 0 else (other, other_cols)
        k = pl.ds(pl.multiple_of(index * spans[0], spans[0]), spans[0])
        part = jnp.dot(
            place[which, :, k], buf[index].reshape(spans[0], half), preferred_element_type=F32
        )
        if start:
            block_ref[:, cols] = part
        else:
            block_ref[:, cols] = block_ref[:, cols] + part

    swaps = {}

    def swap(a, b):
        i, j = turn(three, a, ring), turn(two, b, ring)
        n = a * ring + b
        swaps[a, b] = send_to(own.at[i, j], other.at[i, j], swap_send.at[n], swap_recv.at[n], partner)
        swaps[a, b].start()

    straight = {}

    def onward(b):
        there = own.at[three, turn(two, b, ring)]
        for k, goal in enumerate((plus, minus)):
            copy = send_to(there, there, three_send.at[k, b], three_recv.at[k, b], goal)
            copy.start()
            straight[k, b] = copy

    relays = {}

    def relay(k, b):
        there = own.at[turn(three, -1 if k == 0 else 1, ring), turn(two, b, ring)]
        n = {0: 0, 1: 1, 3: 2, 2: 3}[b]
        copy = send_to(there, there, relay_send.at[n], relay_recv.at[n], plus if k == 0 else minus)
        copy.start()
        relays[b] = copy

    for copy in far:
        copy.wait_recv()
    second = {}
    for d in (1, 3, 2):
        there = own.at[three, two]
        second[d] = send_to(there, there, two_send.at[d - 1], two_recv.at[d - 1], on_two(turn(two, -d, ring)))
        second[d].start()
    onward(0)
    swap(0, 0)
    for c in range(chunks // 2):
        widen(c)
    for d in (1, 3):
        second[d].wait_recv()
        onward(d)
        swap(0, d)
    straight[0, 0].wait_recv()
    relay(0, 0)
    swap(3, 0)
    straight[1, 0].wait_recv()
    swap(1, 0)
    second[2].wait_recv()
    onward(2)
    swap(0, 2)
    add_block(0, three, True)
    straight[0, 1].wait_recv()
    relay(0, 1)
    swap(3, 1)
    straight[1, 3].wait_recv()
    relay(1, 3)
    swap(1, 3)
    straight[1, 1].wait_recv()
    swap(1, 1)
    straight[0, 3].wait_recv()
    swap(3, 3)
    for c in range(chunks // 2, chunks):
        widen(c)
    straight[1, 2].wait_recv()
    relay(1, 2)
    swap(1, 2)
    straight[0, 2].wait_recv()
    swap(3, 2)
    add_block(0, turn(three, 1, ring), False)
    add_block(0, turn(three, -1, ring), False)
    for b in range(ring):
        swaps[0, b].wait_recv()
    add_block(1, two, True)
    for b in (0, 1, 3, 2):
        relays[b].wait_recv()
        swap(2, b)
    add_block(0, turn(three, 2, ring), False)
    for a in (1, 3, 2):
        for b in range(ring):
            swaps[a, b].wait_recv()
        add_block(1, turn(two, a, ring), False)
    for copy in waits + list(second.values()) + list(straight.values()) + list(relays.values()) + list(swaps.values()):
        copy.wait_send()


def solve_kernel(width, scale, shift, block_ref, b_ref, coef_ref, swapped, system):
    size = b_ref.shape[0]
    groups = size // LANES
    base = WIDE - LANES
    col = width - base
    eye = eye_mask()
    tail = block_ref[:, base:]
    lane = lane_of(tail.shape)
    target_cols = jnp.sum(
        jnp.where((lane >= col + 6) & (lane < col + 9), tail, 0.0), axis=1, keepdims=True
    )
    tail = jnp.where(lane < col + 6, tail, 0.0)
    moved = pltpu.roll(tail, 3, 1)
    swap = jnp.where(lane < col, tail, jnp.where(lane < col + 3, 1.0, jnp.where(lane < col + 6, moved, 0.0)))
    plain = block_ref[:, :base].astype(BF16)
    b_ref[:, :base] = plain
    b_ref[:, base:] = tail.astype(BF16)
    swapped[:, :base] = plain
    swapped[:, base:] = swap.astype(BF16)
    inner = lax.dot_general(
        b_ref[...], swapped[...], (((1,), (1,)), ((), ())), preferred_element_type=F32
    )
    system[...] = jnp.exp2(inner * (2.0 * scale * LOG2E))
    for t in range(groups):
        here = slice(t * LANES, (t + 1) * LANES)
        system[here, here] = system[here, here] + jnp.where(eye, shift, 0.0)

    target = jnp.concatenate(
        [to_row(target_cols[t * LANES : (t + 1) * LANES], eye) for t in range(groups)], axis=0
    )
    top = jnp.max(jnp.max(jnp.abs(target), axis=1, keepdims=True), axis=0, keepdims=True)
    top = jnp.where(top > 0.0, top, 1.0)
    target = target / top

    def apply(p):
        rows = []
        for t in range(groups):
            acc = system[t * LANES : (t + 1) * LANES, :LANES] * p[:1, :]
            for u in range(1, groups):
                acc = acc + system[t * LANES : (t + 1) * LANES, u * LANES : (u + 1) * LANES] * p[u : u + 1, :]
            rows.append(to_row(jnp.sum(acc, axis=1, keepdims=True), eye))
        return jnp.concatenate(rows, axis=0)

    first = total(target * target)
    bound = first * 1e-12

    def going(carry):
        step, _, _, _, norm = carry
        return (step < 4 * size) & (jnp.sum(norm - bound) > 0.0)

    def advance(carry):
        step, x, r, p, norm = carry
        q = apply(p)
        alpha = norm / total(p * q)
        x = x + alpha * p
        r = r - alpha * q
        fresh = total(r * r)
        p = r + (fresh / norm) * p
        return step + 1, x, r, p, fresh

    out = lax.while_loop(
        going, advance, (jnp.int32(0), jnp.zeros_like(target), target, target, first)
    )
    coef_ref[...] = out[1] * top


def panel_kernel(
    tile, scale, frames, coef_ref, b_ref, x_ref, res_ref, out_ref, rms_ref,
    columns, line_a, line_b, send_a, recv_a, send_b, recv_b,
):
    rows = x_ref.shape[1]
    size = b_ref.shape[0]
    me, y, z, x, core = position()
    spot_a = z * 2 + core
    spot_b = y * GRID[2] + x
    count_a = line_a.shape[0]
    count_b = line_b.shape[0]

    def peer_a(d):
        v = lax.rem(spot_a + d, count_a)
        return device(y, v // 2, x, lax.rem(v, 2))

    def peer_b(d):
        v = lax.rem(spot_b + d, count_b)
        return device(v // GRID[2], z, lax.rem(v, GRID[2]), core)

    barrier = pltpu.get_barrier_semaphore()

    def greet_a(d, _):
        signal(barrier, peer_a(d))
        return 0

    def greet_b(d, _):
        signal(barrier, peer_b(d))
        return 0

    lax.fori_loop(1, count_a, greet_a, 0)
    lax.fori_loop(1, count_b, greet_b, 0)

    eye = eye_mask()
    for t in range(size // LANES):
        columns[t * LANES : (t + 1) * LANES, :] = jnp.broadcast_to(
            to_column(coef_ref[t : t + 1, :], eye), (LANES, LANES)
        )

    def step(i, _):
        here = pl.ds(pl.multiple_of(i * tile, tile), tile)
        inner = jnp.dot(b_ref[:, :DEEP], x_ref[:, here], preferred_element_type=F32)
        value = jnp.exp2(inner * (2.0 * scale * LOG2E))
        for k in range(tile // LANES):
            change = jnp.sum(value[:, k * LANES : (k + 1) * LANES] * columns[...], axis=0, keepdims=True)
            at = pl.ds(i * (tile // LANES) + k, 1)
            out_ref[at, :] = res_ref[at, :] - change
        return 0

    lax.fori_loop(0, rows // tile, step, 0)
    updated = out_ref[...]
    square = updated * updated
    parts = square[:8, :]
    for t in range(1, square.shape[0] // 8):
        parts = parts + square[t * 8 : (t + 1) * 8, :]
    line_a[spot_a] = jnp.broadcast_to(total(parts), (1, LANES))

    pl.semaphore_wait(barrier, count_a + count_b - 2)

    def exchange(line, spot, send, recv, peer):
        def copy(d):
            return send_to(line.at[spot], line.at[spot], send.at[d - 1], recv.at[d - 1], peer(d))

        def begin(d, _):
            copy(d).start()
            return 0

        def end(d, _):
            copy(d).wait()
            return 0

        lax.fori_loop(1, line.shape[0], begin, 0)
        lax.fori_loop(1, line.shape[0], end, 0)
        out = line[0]
        for k in range(1, line.shape[0]):
            out = out + line[k]
        return out

    line_b[spot_b] = exchange(line_a, spot_a, send_a, recv_a, peer_a)
    whole = exchange(line_b, spot_b, send_b, recv_b, peer_b)
    rms_ref[...] = jnp.sqrt(whole / frames + 1e-06)


VM = pl.BlockSpec(memory_space=pltpu.VMEM)
DMA = pltpu.SemaphoreType.DMA


def gather(idx, features, residual):
    width, local_rows = features.shape
    size = idx.shape[0]
    slots = 2 * GRID[0] * GRID[1] * GRID[2] * MOST
    part = (GRID[0], GRID[2], GRID[1], 2 * MOST, WIDE // 2)
    return pl.pallas_call(
        functools.partial(gather_kernel, local_rows),
        out_shape=(
            jax.ShapeDtypeStruct((DEEP, local_rows), BF16),
            jax.ShapeDtypeStruct((size, WIDE), F32),
        ),
        in_specs=[VM, pl.BlockSpec(memory_space=pl.ANY), VM],
        out_specs=(VM, VM),
        scratch_shapes=[
            pltpu.VMEM((width, local_rows), BF16),
            pltpu.VMEM((2, size, slots), BF16),
            pltpu.VMEM((2, MOST, WIDE), F32),
            pltpu.VMEM(part, BF16),
            pltpu.VMEM(part, BF16),
            DMA((4,)),
            DMA((2,)),
            DMA((GRID[1] - 1,)),
            DMA((GRID[1] - 1,)),
            DMA((3,)),
            DMA((3,)),
            DMA((2, 4)),
            DMA((2, 4)),
            DMA((4,)),
            DMA((4,)),
            DMA((16,)),
            DMA((16,)),
        ],
        compiler_params=pltpu.CompilerParams(
            vmem_limit_bytes=36 << 20, collective_id=0, has_side_effects=True
        ),
        name="gather",
    )(idx.reshape(size // LANES, LANES), features, residual.reshape(local_rows // LANES, LANES))


def solve(block, width, scale):
    size = block.shape[0]
    return pl.pallas_call(
        functools.partial(solve_kernel, width, scale, 0.1),
        out_shape=(
            jax.ShapeDtypeStruct((size, WIDE), BF16),
            jax.ShapeDtypeStruct((size // LANES, LANES), F32),
        ),
        in_specs=[VM],
        out_specs=(VM, VM),
        scratch_shapes=[
            pltpu.VMEM((size, WIDE), BF16),
            pltpu.VMEM((size, size), F32),
        ],
        compiler_params=pltpu.CompilerParams(vmem_limit_bytes=36 << 20),
        name="solve",
    )(block)


def panel(coef, block, wide, residual, scale):
    rows = wide.shape[1]
    size = block.shape[0]
    tile = 256
    return pl.pallas_call(
        functools.partial(panel_kernel, tile, scale, float(rows * lax.axis_size("rows"))),
        out_shape=(
            jax.ShapeDtypeStruct((rows // LANES, LANES), F32),
            jax.ShapeDtypeStruct((1, LANES), F32),
        ),
        in_specs=[VM, VM, VM, VM],
        out_specs=(VM, VM),
        scratch_shapes=[
            pltpu.VMEM((size, LANES), F32),
            pltpu.VMEM((2 * GRID[1], 1, LANES), F32),
            pltpu.VMEM((GRID[0] * GRID[2], 1, LANES), F32),
            DMA((15,)),
            DMA((15,)),
            DMA((15,)),
            DMA((15,)),
        ],
        compiler_params=pltpu.CompilerParams(
            vmem_limit_bytes=36 << 20, collective_id=1, has_side_effects=True
        ),
        name="panel",
    )(coef, block, wide, residual.reshape(rows // LANES, LANES))


def on_device(features, residual, block_index):
    local_rows, width = features.shape
    scale = 2.0 / width
    wide, block = gather(block_index, features.T, residual)
    block, coef = solve(block, width, scale)
    updated, rms = panel(coef, block, wide, residual, scale)
    return (updated.reshape(local_rows), coef.reshape(-1), rms[0, 0])


def solution(mesh):
    in_specs = (P("rows", None), P("rows"), P())
    out_specs = (P("rows"), P(), P())
    return jax.shard_map(
        on_device, mesh=mesh, in_specs=in_specs, out_specs=out_specs, check_vma=False
    )
```

time: 252 us -> 75.6 us (0.30)
  waiting for transfers between devices: 108 us -> 0 us
  blocking collectives: 76.9 us -> 0 us
  Pallas kernels: 30.8 us -> 68.8 us
  between operations: 15.9 us -> 1.82 us
  local copies, waits for them, and re-layouts: 17.2 us -> 4.71 us
    all_gather x1 -> x0, waiting for transfers between devices: 108 us -> none  [on_device(): gathered = lax.all_gather(mine, 'rows', axis=0, tiled=True)]
    psum x1 -> x0, blocking collectives: 76.9 us -> none  [on_device(): square_sum = lax.psum(square[0, 0], 'rows')]
    pallas_call x2 -> x3, Pallas kernels: 30.8 us -> 68.8 us  [the longest x1 30 us: gather(): pl.pallas_call(functools.partial(gather_kernel, local_rows), out_shape=(j...]
    unnamed x11 -> x9, local copies, waits for them, and re-layouts: 10.9 us -> 4.71 us
    gather x2 -> x0, local copies, waits for them, and re-layouts: 4.66 us -> none  [the longest x1 3.3 us: slots_of(): rows = jnp.where(found, features[offset].astype(F32), 0.0)]
  transfers between devices with their start and end apart: 1 -> 0, of which waited for: 1 -> 0; matrix products, arithmetic and copies ran while one was open for 0% -> 0% of each run, Pallas kernels for 0% -> 0%
where the time goes in v2:
time: 75.6 us; the launch traced here: 75.3 us
  Pallas kernels  68.8 us (91%)
  local copies, waits for them, and re-layouts  4.71 us (6%)
  between operations  1.82 us (2%)
    pallas_call x1, Pallas kernels, gather(): pl.pallas_call(functools.partial(gather_kernel, local_rows), out_shape=(j...  30 us
    pallas_call x1, Pallas kernels, panel(): pl.pallas_call(functools.partial(panel_kernel, tile, scale, float(rows *...  19.8 us
    pallas_call x1, Pallas kernels, solve(): pl.pallas_call(functools.partial(solve_kernel, width, scale, 0.1), out_sh...  18.9 us
    unnamed x9, local copies, waits for them, and re-layouts  4.71 us

profile of v2, /device:TPU:1, one launch (start us, length us, event | category | flops | bytes accessed | tf_op | source)
XLA Modules:
  0.0 75.3 jit_solution(14635060921973605080)
XLA Ops:
  0.6 0.0 copy-start
  0.6 2.0 %copy-done = bf16[4096,440]{0,1:T(8,128)(2,1)S(1)} copy-done((bf16[4096,440]{0,1:T(8,128)(2,1)S(1)}, bf16[4096,440]{0,1:T(8,128)(2,1)}, u32[]{:S(2)}) %copy-start) | copy-done | bytes 3604504
  2.7 0.0 copy-start.1
  2.7 0.7 copy-done.1
  3.4 0.0 copy-start.2
  3.4 0.7 copy-done.2
  4.1 30.0 %gather.1 = (bf16[448,4096]{1,0:T(8,128)(2,1)S(1)}, f32[1024,512]{1,0:T(8,128)S(1)}) custom-call(s32[8,128]{1,0:T(8,128)S(1)} %bitcast.11, bf16[440,4096]{1,0:T(8,128)(2,1)S(1)} %bitcast.7, f32[32,128]{1,0:T(8,128)S(1)} %bitcast.8), custom_call_target="tpu_custom_call" | custom-call | tf_op jit(solution)/shard_map/gather/pallas_call | solution.py:486
  34.1 18.9 %solve.1 = (bf16[1024,512]{1,0:T(8,128)(2,1)S(1)}, f32[8,128]{1,0:T(8,128)}) custom-call(f32[1024,512]{1,0:T(8,128)S(1)} %get-tuple-element.9.block_ref), custom_call_target="tpu_custom_call" | custom-call | tf_op jit(solution)/shard_map/solve/pallas_call | solution.py:522
  53.0 0.0 copy-start.3
  53.0 0.7 copy-done.3
  53.7 19.8 %panel.1 = (f32[32,128]{1,0:T(8,128)S(1)}, f32[1,128]{1,0:T(1,128)S(1)}) custom-call(f32[8,128]{1,0:T(8,128)S(1)} %copy-done.3, bf16[1024,512]{1,0:T(8,128)(2,1)S(1)} %get-tuple-element.11.b_ref, bf16[448,4096]{1,0:T(8,128)(2,1)S(1)} %get-tuple-element.12.x_ref, f32[32,128]{1,0:T(8,128)S(1)} %bitcast.9), custom_call_target="tpu_custom_call" | custom-call | tf_op jit(solution)/shard_map/panel/pallas_call | solution.py:543
  73.5 0.6 copy.8
Async XLA Ops:
  0.6 2.0 %copy-start = (bf16[4096,440]{0,1:T(8,128)(2,1)S(1)}, bf16[4096,440]{0,1:T(8,128)(2,1)}, u32[]{:S(2)}) copy-start(bf16[4096,440]{0,1:T(8,128)(2,1)} %param.3) | copy-start | bytes 10813444
  2.7 0.7 copy-start.1
  3.4 0.7 copy-start.2
  53.0 0.7 copy-start.3

commit v3 on v2

--- a/solution.py
+++ b/solution.py
@@ -95,8 +95,8 @@
 
 
 def gather_kernel(
-    local_rows, idx_ref, x_hbm, res_ref, xa_ref, block_ref,
-    xs, place, pair, own, other, load_sem, pair_sem, far_send, far_recv, two_send, two_recv,
+    local_rows, idx_hbm, x_hbm, res_hbm, xa_ref, block_ref,
+    idx_ref, res_ref, small_sem, xs, place, pair, own, other, load_sem, pair_sem, far_send, far_recv, two_send, two_recv,
     three_send, three_recv, relay_send, relay_recv, swap_send, swap_recv,
 ):
     width = xs.shape[0]
@@ -135,18 +135,26 @@
     signal(barrier, plus)
     signal(barrier, minus)
 
+    small = [
+        pltpu.make_async_copy(idx_hbm, idx_ref, small_sem.at[0]),
+        pltpu.make_async_copy(res_hbm, res_ref, small_sem.at[1]),
+    ]
+    for copy in small:
+        copy.start()
     loads = []
     for c in range(chunks):
         here = slice(c * step, (c + 1) * step)
         loads.append(pltpu.make_async_copy(x_hbm.at[:, here], xs.at[:, here], load_sem.at[c]))
         loads[-1].start()
 
+    small[0].wait()
     idx = idx_ref[...]
     offsets = own_offsets(idx, me, local_rows)
     column = stacked(offsets)
     frame = (
         lax.broadcasted_iota(jnp.int32, res_ref.shape, 0) * LANES + lane_of(res_ref.shape)
     ).astype(F32)
+    small[1].wait()
     target = stacked([total(jnp.where(frame == v, res_ref[...], 0.0)) for v in offsets])
     rows = None
     for c in range(chunks):
@@ -325,7 +333,7 @@
         copy.wait_send()
 
 
-def solve_kernel(width, scale, shift, block_ref, b_ref, coef_ref, swapped, system):
+def solve_kernel(width, scale, shift, block_ref, b_ref, coef_ref, columns_ref, swapped, system):
     size = b_ref.shape[0]
     groups = size // LANES
     base = WIDE - LANES
@@ -388,15 +396,19 @@
     out = lax.while_loop(
         going, advance, (jnp.int32(0), jnp.zeros_like(target), target, target, first)
     )
-    coef_ref[...] = out[1] * top
+    coef = out[1] * top
+    coef_ref[...] = coef
+    for t in range(groups):
+        columns_ref[t * LANES : (t + 1) * LANES, :] = jnp.broadcast_to(
+            to_column(coef[t : t + 1, :], eye), (LANES, LANES)
+        )
 
 
 def panel_kernel(
-    tile, scale, frames, coef_ref, b_ref, x_ref, res_ref, out_ref, rms_ref,
-    columns, line_a, line_b, send_a, recv_a, send_b, recv_b,
+    tile, scale, frames, columns, b_ref, x_ref, res_hbm, out_ref, rms_ref,
+    res_ref, res_sem, line_a, line_b, send_a, recv_a, send_b, recv_b,
 ):
     rows = x_ref.shape[1]
-    size = b_ref.shape[0]
     me, y, z, x, core = position()
     spot_a = z * 2 + core
     spot_b = y * GRID[2] + x
@@ -424,11 +436,9 @@
     lax.fori_loop(1, count_a, greet_a, 0)
     lax.fori_loop(1, count_b, greet_b, 0)
 
-    eye = eye_mask()
-    for t in range(size // LANES):
-        columns[t * LANES : (t + 1) * LANES, :] = jnp.broadcast_to(
-            to_column(coef_ref[t : t + 1, :], eye), (LANES, LANES)
-        )
+    load = pltpu.make_async_copy(res_hbm, res_ref, res_sem)
+    load.start()
+    load.wait()
 
     def step(i, _):
         here = pl.ds(pl.multiple_of(i * tile, tile), tile)
@@ -475,7 +485,12 @@
 
 
 VM = pl.BlockSpec(memory_space=pltpu.VMEM)
+HBM = pl.BlockSpec(memory_space=pltpu.HBM)
 DMA = pltpu.SemaphoreType.DMA
+
+
+def in_hbm(value):
+    return pltpu.with_memory_space_constraint(value, pltpu.HBM)
 
 
 def gather(idx, features, residual):
@@ -489,9 +504,12 @@
             jax.ShapeDtypeStruct((DEEP, local_rows), BF16),
             jax.ShapeDtypeStruct((size, WIDE), F32),
         ),
-        in_specs=[VM, pl.BlockSpec(memory_space=pl.ANY), VM],
+        in_specs=[HBM, HBM, HBM],
         out_specs=(VM, VM),
         scratch_shapes=[
+            pltpu.VMEM((size // LANES, LANES), jnp.int32),
+            pltpu.VMEM((local_rows // LANES, LANES), F32),
+            DMA((2,)),
             pltpu.VMEM((width, local_rows), BF16),
             pltpu.VMEM((2, size, slots), BF16),
             pltpu.VMEM((2, MOST, WIDE), F32),
@@ -514,7 +532,11 @@
             vmem_limit_bytes=36 << 20, collective_id=0, has_side_effects=True
         ),
         name="gather",
-    )(idx.reshape(size // LANES, LANES), features, residual.reshape(local_rows // LANES, LANES))
+    )(
+        in_hbm(idx.reshape(size // LANES, LANES)),
+        in_hbm(features),
+        in_hbm(residual.reshape(local_rows // LANES, LANES)),
+    )
 
 
 def solve(block, width, scale):
@@ -524,9 +546,10 @@
         out_shape=(
             jax.ShapeDtypeStruct((size, WIDE), BF16),
             jax.ShapeDtypeStruct((size // LANES, LANES), F32),
+            jax.ShapeDtypeStruct((size, LANES), F32),
         ),
         in_specs=[VM],
-        out_specs=(VM, VM),
+        out_specs=(VM, VM, VM),
         scratch_shapes=[
             pltpu.VMEM((size, WIDE), BF16),
             pltpu.VMEM((size, size), F32),
@@ -536,20 +559,20 @@
     )(block)
 
 
-def panel(coef, block, wide, residual, scale):
+def panel(columns, block, wide, residual, scale):
     rows = wide.shape[1]
-    size = block.shape[0]
-    tile = 256
+    tile = 1024
     return pl.pallas_call(
         functools.partial(panel_kernel, tile, scale, float(rows * lax.axis_size("rows"))),
         out_shape=(
             jax.ShapeDtypeStruct((rows // LANES, LANES), F32),
             jax.ShapeDtypeStruct((1, LANES), F32),
         ),
-        in_specs=[VM, VM, VM, VM],
+        in_specs=[VM, VM, VM, HBM],
         out_specs=(VM, VM),
         scratch_shapes=[
-            pltpu.VMEM((size, LANES), F32),
+            pltpu.VMEM((rows // LANES, LANES), F32),
+            DMA,
             pltpu.VMEM((2 * GRID[1], 1, LANES), F32),
             pltpu.VMEM((GRID[0] * GRID[2], 1, LANES), F32),
             DMA((15,)),
@@ -561,15 +584,15 @@
             vmem_limit_bytes=36 << 20, collective_id=1, has_side_effects=True
         ),
         name="panel",
-    )(coef, block, wide, residual.reshape(rows // LANES, LANES))
+    )(columns, block, wide, in_hbm(residual.reshape(rows // LANES, LANES)))
 
 
 def on_device(features, residual, block_index):
     local_rows, width = features.shape
     scale = 2.0 / width
     wide, block = gather(block_index, features.T, residual)
-    block, coef = solve(block, width, scale)
-    updated, rms = panel(coef, block, wide, residual, scale)
+    block, coef, columns = solve(block, width, scale)
+    updated, rms = panel(columns, block, wide, residual, scale)
     return (updated.reshape(local_rows), coef.reshape(-1), rms[0, 0])
 
 

time: 75.6 us -> 68.4 us (0.905); the launches traced: 75.3 us -> 69.2 us
  local copies, waits for them, and re-layouts: 4.71 us -> 0.61 us
  Pallas kernels: 68.8 us -> 66.8 us
    pallas_call x1, Pallas kernels: 19.8 us -> 15.6 us  [panel(): pl.pallas_call(functools.partial(panel_kernel, tile, scale, float(rows *...]
    unnamed x9 -> x1, local copies, waits for them, and re-layouts: 4.71 us -> 0.61 us
    pallas_call x1, Pallas kernels: 30 us -> 31.7 us  [gather(): pl.pallas_call(functools.partial(gather_kernel, local_rows), out_shape=(j...]
where the time goes in v3:
time: 68.4 us; the launch traced here: 69.2 us
  Pallas kernels  66.8 us (98%)
  between operations  1.81 us (3%)
    pallas_call x1, Pallas kernels, gather(): pl.pallas_call(functools.partial(gather_kernel, local_rows), out_shape=(j...  31.7 us
    pallas_call x1, Pallas kernels, solve(): pl.pallas_call(functools.partial(solve_kernel, width, scale, 0.1), out_sh...  19.5 us
    pallas_call x1, Pallas kernels, panel(): pl.pallas_call(functools.partial(panel_kernel, tile, scale, float(rows *...  15.6 us

profile of v3, /device:TPU:1, one launch (start us, length us, event | category | flops | bytes accessed | tf_op | source)
XLA Modules:
  0.0 69.2 jit_solution(15553925556496403824)
XLA Ops:
  0.6 31.7 %gather.1 = (bf16[448,4096]{1,0:T(8,128)(2,1)S(1)}, f32[1024,512]{1,0:T(8,128)S(1)}) custom-call(s32[8,128]{1,0:T(8,128)} %bitcast.12, bf16[440,4096]{1,0:T(8,128)(2,1)} %bitcast.9, f32[32,128]{1,0:T(8,128)} %bitcast.10), custom_call_target="tpu_custom_call" | custom-call | tf_op jit(solution)/shard_map/gather/pallas_call | solution.py:501
  32.3 19.5 %solve.1 = (bf16[1024,512]{1,0:T(8,128)(2,1)S(1)}, f32[8,128]{1,0:T(8,128)}, f32[1024,128]{1,0:T(8,128)S(1)}) custom-call(f32[1024,512]{1,0:T(8,128)S(1)} %get-tuple-element.10.block_ref), custom_call_target="tpu_custom_call" | custom-call | tf_op jit(solution)/shard_map/solve/pallas_call | solution.py:544
  51.8 15.6 %panel.1 = (f32[32,128]{1,0:T(8,128)S(1)}, f32[1,128]{1,0:T(1,128)S(1)}) custom-call(f32[1024,128]{1,0:T(8,128)S(1)} %get-tuple-element.11.columns, bf16[1024,512]{1,0:T(8,128)(2,1)S(1)} %get-tuple-element.12.b_ref, bf16[448,4096]{1,0:T(8,128)(2,1)S(1)} %get-tuple-element.13.x_ref, f32[32,128]{1,0:T(8,128)} %bitcast.11), custom_call_target="tpu_custom_call" | custom-call | tf_op jit(solution)/shard_map/panel/pallas_call | solution.py:565
  67.4 0.6 copy.8
